TPU v7x, 256 devices: a whole 4x4x8 slice. The times are simulated.
256 devices in a mesh: grp: 8 (over x, core), vocab: 32 (over y, z).
Axes of the slice: x: 4, y: 4, z: 8, core: 2. Of those that a mesh axis runs over, the one named last changes fastest.
Arguments:
- hidden: bfloat16 [1024, 16384], P('grp', 'vocab'), may hold values from -6 to 6
- flags: int32 [1024, 1], P('grp'), may hold values from 0 to 8; in each aligned block of 128 rows (0 to 127, 128 to 255, ...) at most 16 rows name the same one
- targets: int32 [1024], P('grp'), may hold values from 0 to 65535
- head: bfloat16 [16384, 65536], P('grp', 'vocab'), may hold values from -0.140625 to 0.140625
- lengths: int32 [8, 8], P('grp'), may hold values from 1 to 64, 128 in all within a row
Outputs:
- token_scores: float32 [1024], P('grp')
- doc_scores: float32 [8, 8], P('grp')
Inputs may be any that keep to these rules, and one draw needn't show every extreme that they name: `flags`: A value below 8 names the scorer group of a scored row. Within the 128 rows of one shard no value occurs more than 16 times, and in every draw some value occurs exactly 16 times in some shard.
All inputs are finite; a program needn't handle non-finite values.
Results may differ from a plain program's by a relative error of at most 0.0003.
Values may be sent and summed in bfloat16 or wider, within the bound.
A program may use at most 128 MiB of HBM per device.

v0:
```python
import jax
import jax.numpy as jnp
from jax import lax
from jax.sharding import PartitionSpec as P


def combined_all(part, axis, combine):
    gathered = jax.tree.map(lambda a: lax.all_gather(a, axis), part)

    def take(source):
        return jax.tree.map(lambda a: lax.dynamic_index_in_dim(a, source, 0, False), gathered)

    return lax.fori_loop(
        1, lax.axis_size(axis), lambda source, state: combine(state, take(source)), take(0)
    )


def slot_table(flag_col, groups, capacity, shard_rows):
    values = jnp.arange(groups + 1, dtype=jnp.int32)
    onehot = (flag_col[:, None] == values[None, :]).astype(jnp.int32)
    ranking = jnp.sum((jnp.cumsum(onehot, axis=0) - 1) * onehot, axis=1)
    where_to = jnp.where(flag_col < groups, flag_col * capacity + ranking, groups * capacity)
    table = jnp.full((groups * capacity + 1,), -1, jnp.int32)
    table = table.at[where_to].set(jnp.arange(shard_rows, dtype=jnp.int32))
    return table[: groups * capacity]


def combine_stats(left, right):
    row_max = jnp.maximum(left[0], right[0])
    left_gap = left[0] - row_max
    right_gap = right[0] - row_max
    left_fac = jnp.exp(left_gap)
    right_fac = jnp.exp(right_gap)
    row_total = left_fac * left[1] + right_fac * right[1]
    first_mom = left_fac * (left[2] + left_gap * left[1]) + right_fac * (
        right[2] + right_gap * right[1]
    )
    second_mom = left_fac * (left[3] + 2.0 * left_gap * left[2] + left_gap * left_gap * left[1])
    second_mom = second_mom + right_fac * (
        right[3] + 2.0 * right_gap * right[2] + right_gap * right_gap * right[1]
    )
    return (row_max, row_total, first_mom, second_mom)


def local_stats(logits, target_ids, columns, axis):
    row_max = jnp.max(logits, axis=axis)
    shifted = logits - jnp.expand_dims(row_max, axis)
    scaled = jnp.exp(shifted)
    row_total = jnp.sum(scaled, axis=axis)
    first_mom = jnp.sum(scaled * shifted, axis=axis)
    second_mom = jnp.sum(scaled * shifted * shifted, axis=axis)
    is_target = target_ids[:, None] == columns[None, :]
    target_val = jnp.sum(jnp.where(is_target, logits, jnp.float32(0.0)), axis=axis)
    return (row_max, row_total, first_mom, second_mom, target_val)


def final_scores(target_ids, row_max, row_total, first_mom, second_mom, target_val):
    mean_shift = first_mom / row_total
    row_var = second_mom / row_total - mean_shift * mean_shift
    return jnp.where(
        target_ids >= 0,
        (target_val - row_max - mean_shift) / jnp.sqrt(jnp.maximum(row_var, 1.0)),
        jnp.float32(0.0),
    )


def shards(hidden, flags, targets, head, lengths):
    groups = lax.axis_size("grp")
    shard_rows = hidden.shape[0]
    capacity = shard_rows // groups
    vocab_dev = head.shape[1]
    my_vocab = lax.axis_index("vocab")
    flag_col = flags[:, 0]
    table = slot_table(flag_col, groups, capacity, shard_rows)
    is_live = table >= 0
    safe_rows = jnp.maximum(table, 0)
    pieces = jnp.where(is_live[:, None], hidden[safe_rows], jnp.zeros((), jnp.bfloat16))
    slot_targets = jnp.where(is_live, targets[safe_rows], -1)
    arrived = lax.all_to_all(
        pieces.reshape(groups, capacity, pieces.shape[1]),
        "grp",
        split_axis=0,
        concat_axis=0,
        tiled=True,
    )
    full_rows = lax.all_gather(
        arrived.reshape(shard_rows, pieces.shape[1]), "vocab", axis=1, tiled=True
    )
    block_rows = lax.all_to_all(full_rows, "grp", split_axis=1, concat_axis=0, tiled=True)
    target_ids = lax.all_to_all(
        slot_targets.reshape(groups, capacity), "grp", split_axis=0, concat_axis=0, tiled=True
    ).reshape(shard_rows)
    logits = lax.psum_scatter(
        jnp.dot(block_rows, head, preferred_element_type=jnp.float32),
        "grp",
        scatter_dimension=0,
        tiled=True,
    )
    columns = my_vocab * vocab_dev + jnp.arange(vocab_dev, dtype=jnp.int32)
    row_max, row_total, first_mom, second_mom, target_val = local_stats(
        logits, target_ids, columns, 1
    )
    row_max, row_total, first_mom, second_mom = combined_all(
        (row_max, row_total, first_mom, second_mom), "vocab", combine_stats
    )
    target_val = lax.psum(target_val, "vocab")
    token_scores = final_scores(target_ids, row_max, row_total, first_mom, second_mom, target_val)
    returned = lax.all_to_all(
        token_scores.reshape(groups, capacity), "grp", split_axis=0, concat_axis=0, tiled=True
    ).reshape(shard_rows)
    row_val = (
        jnp.zeros((shard_rows + 1,), jnp.float32)
        .at[jnp.where(is_live, table, shard_rows)]
        .set(returned)[:shard_rows]
    )
    flagged = (flag_col < groups).astype(jnp.float32)
    doc_ends = jnp.cumsum(lengths[0])
    doc_starts = doc_ends - lengths[0]
    positions = jnp.arange(shard_rows, dtype=jnp.int32)
    membership = (
        (positions[None, :] >= doc_starts[:, None]) & (positions[None, :] < doc_ends[:, None])
    ).astype(jnp.float32)
    sums = jnp.sum(membership * row_val[None, :], axis=1)
    counts = jnp.sum(membership * flagged[None, :], axis=1)
    doc_means = (sums / jnp.maximum(counts, 1.0))[None, :]
    return (token_scores, doc_means)


def solution(mesh):
    placed = (P("grp", "vocab"), P("grp", None), P("grp"), P("grp", "vocab"), P("grp", None))
    return jax.shard_map(
        shards, mesh=mesh, in_specs=placed, out_specs=(P("grp"), P("grp", None)), check_vma=False
    )
```

profile of v0, /device:TPU:1, one launch (start us, length us, event | category | flops | bytes accessed | tf_op | source)
XLA Modules:
  0.0 488.9 jit_solution(7191298796290074408)
XLA Ops:
  7.2 0.0 copy-start
  7.2 0.0 all-gather.10.cloned.1.call-start
  7.2 0.8 fusion.12
  8.0 0.2 reduce_window_sum.18
  8.2 0.8 select_reduce_fusion.1
  9.0 0.7 fusion.19
  9.7 1.0 scatter_custom_fusion
  10.7 0.1 ge.36
  10.8 0.0 copy-done
  10.8 0.9 gather_fusion.1
  11.6 0.1 broadcast_select_fusion
  11.7 11.6 %all_to_all.39 = bf16[8,16,512]{2,1,0:T(8,128)(2,1)} all-to-all(bf16[8,16,512]{2,1,0:T(8,128)(2,1)S(1)} %broadcast_select_fusion), channel_id=1, replica_groups=mesh['grp'=8,'vocab'=32] {'grp'}, dimensions={0} | all-to-all | bytes 262144 | tf_op jit(solution)/shard_map/all_to_all | solution.py:79
  23.3 0.0 all-gather.10.cloned.1.call-update
  23.3 0.0 reduce-scatter.2.cloned.1.call-start
  23.4 80.8 %all-gather.10.cloned.1.call-done = bf16[128,16384]{1,0:T(8,128)(2,1)} async-done(((bf16[128,512]{1,0:T(8,128)(2,1)}), bf16[128,16384]{1,0:T(8,128)(2,1)}) %all-gather.10.cloned.1.call-update) | async-done | bytes 4194320 | tf_op jit(solution)/shard_map/all_gather | solution.py:86
  104.2 6.4 %copy.16 = bf16[128,16384]{0,1:T(8,128)(2,1)} copy(bf16[128,16384]{1,0:T(8,128)(2,1)} %all-gather.10.cloned.1.call-done) | data formatting | bytes 8388608 | tf_op jit(solution)/shard_map/all_gather | solution.py:86
  110.6 57.6 %all_to_all.40 = bf16[128,8,2048]{0,2,1:T(8,128)(2,1)} all-to-all(bf16[128,8,2048]{0,2,1:T(8,128)(2,1)} %bitcast.91), channel_id=1, replica_groups=mesh['grp'=8,'vocab'=32] {'grp'}, dimensions={1} | all-to-all | bytes 8388608 | tf_op jit(solution)/shard_map/all_to_all | solution.py:89
  168.2 6.5 %copy.17 = bf16[8,128,2048]{2,1,0:T(8,128)(2,1)} copy(bf16[8,128,2048]{1,2,0:T(8,128)(2,1)} %bitcast.92) | data formatting | bytes 8388608 | tf_op jit(solution)/shard_map/all_to_all | solution.py:89
  174.6 14.4 %fusion.21 = f32[1024,2048]{1,0:T(8,128)} fusion(bf16[1024,2048]{1,0:T(8,128)(2,1)} %bitcast.93, bf16[2048,2048]{1,0:T(8,128)(2,1)} %param.10), kind=kOutput, calls=%fused_computation.58 | convolution fusion | flops 8589934592 | bytes 20971520 | tf_op jit(solution)/shard_map/dot_general | solution.py:94
  189.1 0.0 reduce-scatter.2.cloned.1.call-update
  189.1 0.6 copy-done.1
  189.7 1.2 gather_fusion
  191.0 0.7 select_n.65
  191.6 4.2 all-to-all-start
  195.9 0.0 copy-done.4
  195.9 0.2 reduce-window.7
  196.1 4.4 all-to-all-done
  200.5 0.5 broadcast.131
  201.0 0.7 reduce.6
  201.7 0.1 reshape.121
  201.7 40.7 %reduce-scatter.2.cloned.1.call-done = f32[128,2048]{1,0:T(8,128)} async-done(((f32[1024,2048]{1,0:T(8,128)}), f32[128,2048]{1,0:T(8,128)}) %reduce-scatter.2.cloned.1.call-update) | async-done | bytes 1048592 | tf_op jit(solution)/shard_map/reduce_scatter | solution.py:93
  242.4 1.4 reduce_max.9
  243.8 31.7 %all-gather.4 = f32[32,1,128]{2,1,0:T(1,128)S(1)} all-gather(f32[1,1,128]{2,1,0:T(1,128)S(1)} %bitcast.100), channel_id=2, replica_groups=mesh['grp'=8,'vocab'=32] {'vocab'}, dimensions={0}, use_global_device_ids=true | all-gather | bytes 16896 | tf_op jit(solution)/shard_map/all_gather | solution.py:8
  275.4 1.7 fusion.11
  277.2 27.1 %all-gather.5 = f32[32,1,128]{2,1,0:T(1,128)S(1)} all-gather(f32[1,1,128]{2,1,0:T(1,128)S(1)} %bitcast.103), channel_id=3, replica_groups=mesh['grp'=8,'vocab'=32] {'vocab'}, dimensions={0}, use_global_device_ids=true | all-gather | bytes 16896 | tf_op jit(solution)/shard_map/all_gather | solution.py:8
  304.3 28.7 %all-gather.6 = f32[32,1,128]{2,1,0:T(1,128)S(1)} all-gather(f32[1,1,128]{2,1,0:T(1,128)S(1)} %bitcast.102), channel_id=4, replica_groups=mesh['grp'=8,'vocab'=32] {'vocab'}, dimensions={0}, use_global_device_ids=true | all-gather | bytes 16896 | tf_op jit(solution)/shard_map/all_gather | solution.py:8
  333.0 27.2 %all-gather.7 = f32[32,1,128]{2,1,0:T(1,128)S(1)} all-gather(f32[1,1,128]{2,1,0:T(1,128)S(1)} %bitcast.101), channel_id=5, replica_groups=mesh['grp'=8,'vocab'=32] {'vocab'}, dimensions={0}, use_global_device_ids=true | all-gather | bytes 16896 | tf_op jit(solution)/shard_map/all_gather | solution.py:8
  360.2 2.7 while.21
  362.9 56.7 %psum.7 = f32[128]{0:T(128)S(1)} all-reduce(f32[128]{0:T(128)S(1)} %get-tuple-element.232), channel_id=1, replica_groups=mesh['grp'=8,'vocab'=32] {'vocab'}, use_global_device_ids=true, to_apply=%region_5.6 | all-reduce | flops 128 | bytes 1024 | tf_op jit(solution)/shard_map/psum | solution.py:106
  419.6 0.7 all_to_all.33
  420.3 54.2 %all-to-all-start.3 = ((f32[8,1,16]{2,1,0:T(1,128)}), f32[8,1,16]{2,1,0:T(1,128)S(1)}, u32[]{:S(2)}, u32[]{:S(2)}) async-start(f32[8,1,16]{2,1,0:T(1,128)} %bitcast.28), calls=%async_computation.4 | async-start | bytes 8192 | tf_op jit(solution)/shard_map/all_to_all | solution.py:108
  474.5 4.6 all-to-all-done.3
  479.1 0.5 broadcast.132
  479.6 0.7 reduce.7
  480.3 0.1 reshape.155
  480.3 1.0 scatter_custom_fusion.1
  481.3 0.2 select_reduce_fusion.2
  481.5 0.5 fusion.18
  (113 shorter events, 1.8 us)
Async XLA Ops:
  7.2 3.6 copy-start
  7.2 97.0 %all-gather.10.cloned.1.call-start = ((), (), s32[]{:S(2)}) async-start(), calls=%async_computation.5 | async-start | bytes 4325376 | tf_op jit(solution)/shard_map/all_gather | solution.py:86
  23.3 219.1 %reduce-scatter.2.cloned.1.call-start = ((), (), s32[]{:S(2)}) async-start(), calls=%async_computation.6 | async-start | bytes 9437184 | tf_op jit(solution)/shard_map/reduce_scatter | solution.py:93
  189.1 0.7 copy-start.1
  189.1 6.8 %copy-start.4 = (s32[1,8]{1,0:T(1,128)S(1)}, s32[1,8]{1,0:T(1,128)}, u32[]{:S(2)}) copy-start(s32[1,8]{1,0:T(1,128)} %param.11) | copy-start | bytes 100
  189.1 285.4 %copy-start.2 = (s32[128,1]{0,1:T(1,128)S(1)}, s32[128,1]{0,1:T(1,128)}, u32[]{:S(2)}) copy-start(s32[128,1]{0,1:T(1,128)} %param.8) | copy-start | bytes 1540
  191.6 8.8 %all-to-all-start = ((s32[8,1,16]{2,1,0:T(1,128)}), s32[8,1,16]{2,1,0:T(1,128)S(1)}, u32[]{:S(2)}, u32[]{:S(2)}) async-start(s32[8,1,16]{2,1,0:T(1,128)} %bitcast.7), calls=%async_computation | async-start | bytes 8192 | tf_op jit(solution)/shard_map/all_to_all | solution.py:90
  419.6 62.5 %copy-start.3 = (f32[128]{0:T(128)}, f32[128]{0:T(128)S(1)}, u32[]{:S(2)}) copy-start(f32[128]{0:T(128)S(1)} %compare_select_fusion.2) | copy-start | bytes 1540
  420.3 58.8 %all-to-all-start.3 = ((f32[8,1,16]{2,1,0:T(1,128)}), f32[8,1,16]{2,1,0:T(1,128)S(1)}, u32[]{:S(2)}, u32[]{:S(2)}) async-start(f32[8,1,16]{2,1,0:T(1,128)} %bitcast.28), calls=%async_computation.4 | async-start | bytes 8192 | tf_op jit(solution)/shard_map/all_to_all | solution.py:108
Sparse Core Ops, SparseCore 0:
  23.4 80.6 all-gather.9
  189.2 53.1 reduce-scatter.1
where the time goes:
time: 490 us; the launch traced here: 489 us
  blocking collectives  241 us (49%)
  waiting for transfers between devices  131 us (27%)
  starting transfers between devices  58.5 us (12%)
  local copies, waits for them, and re-layouts  20.2 us (4%)
  matrix products  14.4 us (3%)
  between operations  14.2 us (3%)
  other arithmetic  9.6 us (2%)
    all_gather x4, blocking collectives, combined_all(): gathered = jax.tree.map(lambda a: lax.all_gather(a, axis), part)  115 us
    all_gather x1, waiting for transfers between devices, shards(): lax.all_gather(arrived.reshape(shard_rows, pieces.shape[1]), 'vocab', axi...  80.8 us
    all_to_all x1, blocking collectives, shards(): lax.all_to_all(full_rows, 'grp', split_axis=1, concat_axis=0, tiled=True)  57.6 us
    psum x1, blocking collectives, shards(): target_val = lax.psum(target_val, 'vocab')  56.7 us
    all_to_all x1, starting transfers between devices, shards(): lax.all_to_all(token_scores.reshape(groups, capacity), 'grp', split_axis=...  54.2 us
    reduce_scatter x1, waiting for transfers between devices, shards(): lax.psum_scatter(jnp.dot(block_rows, head, preferred_element_type=jnp.flo...  40.7 us
    dot_general x1, matrix products, shards(): jnp.dot(block_rows, head, preferred_element_type=jnp.float32)  14.4 us
    all_to_all x1, blocking collectives, shards(): lax.all_to_all(pieces.reshape(groups, capacity, pieces.shape[1]), 'grp',...  11.6 us
  transfers between devices with their start and end apart: 4, of which 4 were waited for; matrix products, arithmetic and copies ran while one was open for 1% of the time, Pallas kernels for 0%

commit v1 on v0

--- a/solution.py
+++ b/solution.py
@@ -2,6 +2,7 @@
 import jax.numpy as jnp
 from jax import lax
 from jax.sharding import PartitionSpec as P
+from jax.lax import all_to_all, axis_size
 
 
 def combined_all(part, axis, combine):
@@ -83,9 +84,13 @@
         concat_axis=0,
         tiled=True,
     )
-    full_rows = lax.all_gather(
-        arrived.reshape(shard_rows, pieces.shape[1]), "vocab", axis=1, tiled=True
-    )
+
+    def draft_strings(vec, axis_id):
+        even = jnp.concatenate(axis_size(axis_id) * [vec], axis=1)
+        formed = all_to_all(even, axis_id, concat_axis=1, split_axis=1, tiled=True)
+        return formed
+
+    full_rows = draft_strings(arrived.reshape(shard_rows, pieces.shape[1]), "vocab")
     block_rows = lax.all_to_all(full_rows, "grp", split_axis=1, concat_axis=0, tiled=True)
     target_ids = lax.all_to_all(
         slot_targets.reshape(groups, capacity), "grp", split_axis=0, concat_axis=0, tiled=True

time: 490 us -> 502 us (1.024)
  blocking collectives: 241 us -> 343 us
  waiting for transfers between devices: 131 us -> 45.9 us
  local copies, waits for them, and re-layouts: 20.2 us -> 14.9 us
    all_to_all x0 -> x1, blocking collectives: none -> 103 us  [draft_strings(): formed = all_to_all(even, axis_id, concat_axis=1, split_axis=1, tiled=True)]
    all_gather x1 -> x0, waiting for transfers between devices: 80.8 us -> none  [shards(): lax.all_gather(arrived.reshape(shard_rows, pieces.shape[1]), 'vocab', axi...]
    all_gather x1 -> x0, local copies, waits for them, and re-layouts: 6.37 us -> none  [shards(): lax.all_gather(arrived.reshape(shard_rows, pieces.shape[1]), 'vocab', axi...]
  transfers between devices with their start and end apart: 4 -> 3, of which waited for: 4 -> 3; matrix products, arithmetic and copies ran while one was open for 1% -> 1% of each run, Pallas kernels for 0% -> 0%
where the time goes in v1:
time: 502 us; the launch traced here: 501 us
  blocking collectives  343 us (68%)
  starting transfers between devices  58.5 us (12%)
  waiting for transfers between devices  45.9 us (9%)
  local copies, waits for them, and re-layouts  14.9 us (3%)
  matrix products  14.4 us (3%)
  between operations  14.2 us (3%)
  other arithmetic  9.59 us (2%)
    all_gather x4, blocking collectives, combined_all(): gathered = jax.tree.map(lambda a: lax.all_gather(a, axis), part)  115 us
    all_to_all x1, blocking collectives, draft_strings(): formed = all_to_all(even, axis_id, concat_axis=1, split_axis=1, tiled=True)  103 us
    all_to_all x1, blocking collectives, shards(): lax.all_to_all(full_rows, 'grp', split_axis=1, concat_axis=0, tiled=True)  57.5 us
    psum x1, blocking collectives, shards(): target_val = lax.psum(target_val, 'vocab')  56.7 us
    all_to_all x1, starting transfers between devices, shards(): lax.all_to_all(token_scores.reshape(groups, capacity), 'grp', split_axis=...  54.2 us
    reduce_scatter x1, waiting for transfers between devices, shards(): lax.psum_scatter(jnp.dot(block_rows, head, preferred_element_type=jnp.flo...  36.9 us
    dot_general x1, matrix products, shards(): jnp.dot(block_rows, head, preferred_element_type=jnp.float32)  14.4 us
    all_to_all x1, blocking collectives, shards(): lax.all_to_all(pieces.reshape(groups, capacity, pieces.shape[1]), 'grp',...  10.9 us
  transfers between devices with their start and end apart: 3, of which 3 were waited for; matrix products, arithmetic and copies ran while one was open for 1% of the time, Pallas kernels for 0%

profile of v1, /device:TPU:1, one launch (start us, length us, event | category | flops | bytes accessed | tf_op | source)
XLA Modules:
  0.0 501.2 jit_solution(1470044901767615267)
XLA Ops:
  7.2 0.0 copy-start
  7.2 0.0 reduce-scatter.2.cloned.1.call-start
  7.2 0.8 fusion.12
  8.0 0.2 reduce_window_sum.18
  8.2 0.8 select_reduce_fusion.1
  9.0 0.7 fusion.19
  9.7 1.0 scatter_custom_fusion
  10.7 0.1 ge.36
  10.8 0.0 copy-done
  10.8 0.9 gather_fusion.1
  11.6 0.1 broadcast_select_fusion
  11.7 10.9 %all_to_all.45 = bf16[8,16,512]{2,1,0:T(8,128)(2,1)S(1)} all-to-all(bf16[8,16,512]{2,1,0:T(8,128)(2,1)S(1)} %broadcast_select_fusion), channel_id=1, replica_groups=mesh['grp'=8,'vocab'=32] {'grp'}, dimensions={0} | all-to-all | bytes 262144 | tf_op jit(solution)/shard_map/all_to_all | solution.py:80
  22.6 0.1 copy.14
  22.7 0.9 concatenate.7
  23.7 103.1 %all_to_all.46 = bf16[128,32,512]{0,2,1:T(8,128)(2,1)S(1)} all-to-all(bf16[128,32,512]{0,2,1:T(8,128)(2,1)S(1)} %concatenate.7), channel_id=1, replica_groups=mesh['grp'=8,'vocab'=32] {'vocab'}, dimensions={1} | all-to-all | bytes 8388608 | tf_op jit(solution)/shard_map/all_to_all | solution.py:90
  126.8 57.5 %all_to_all.47 = bf16[128,8,2048]{0,2,1:T(8,128)(2,1)} all-to-all(bf16[128,8,2048]{0,2,1:T(8,128)(2,1)S(1)} %bitcast.91), channel_id=1, replica_groups=mesh['grp'=8,'vocab'=32] {'grp'}, dimensions={1} | all-to-all | bytes 8388608 | tf_op jit(solution)/shard_map/all_to_all | solution.py:94
  184.3 6.5 %copy.15 = bf16[8,128,2048]{2,1,0:T(8,128)(2,1)} copy(bf16[8,128,2048]{1,2,0:T(8,128)(2,1)} %bitcast.92) | data formatting | bytes 8388608 | tf_op jit(solution)/shard_map/all_to_all | solution.py:94
  190.8 14.4 %fusion.21 = f32[1024,2048]{1,0:T(8,128)} fusion(bf16[1024,2048]{1,0:T(8,128)(2,1)} %bitcast.93, bf16[2048,2048]{1,0:T(8,128)(2,1)} %param.10), kind=kOutput, calls=%fused_computation.58 | convolution fusion | flops 8589934592 | bytes 20971520 | tf_op jit(solution)/shard_map/dot_general | solution.py:99
  205.2 0.0 reduce-scatter.2.cloned.1.call-update
  205.2 0.6 copy-done.1
  205.8 1.2 gather_fusion
  207.1 0.7 select_n.65
  207.8 4.3 all-to-all-start
  212.0 0.0 copy-done.4
  212.0 0.2 reduce-window.7
  212.2 4.4 all-to-all-done
  216.6 0.5 broadcast.132
  217.1 0.7 reduce.6
  217.8 0.1 reshape.188
  217.9 36.9 %reduce-scatter.2.cloned.1.call-done = f32[128,2048]{1,0:T(8,128)} async-done(((f32[1024,2048]{1,0:T(8,128)}), f32[128,2048]{1,0:T(8,128)}) %reduce-scatter.2.cloned.1.call-update) | async-done | bytes 1048592 | tf_op jit(solution)/shard_map/reduce_scatter | solution.py:98
  254.7 1.4 reduce_max.9
  256.1 31.6 %all-gather.4 = f32[32,1,128]{2,1,0:T(1,128)S(1)} all-gather(f32[1,1,128]{2,1,0:T(1,128)S(1)} %bitcast.100), channel_id=2, replica_groups=mesh['grp'=8,'vocab'=32] {'vocab'}, dimensions={0}, use_global_device_ids=true | all-gather | bytes 16896 | tf_op jit(solution)/shard_map/all_gather | solution.py:9
  287.7 1.7 fusion.11
  289.5 27.1 %all-gather.5 = f32[32,1,128]{2,1,0:T(1,128)S(1)} all-gather(f32[1,1,128]{2,1,0:T(1,128)S(1)} %bitcast.103), channel_id=3, replica_groups=mesh['grp'=8,'vocab'=32] {'vocab'}, dimensions={0}, use_global_device_ids=true | all-gather | bytes 16896 | tf_op jit(solution)/shard_map/all_gather | solution.py:9
  316.6 28.8 %all-gather.6 = f32[32,1,128]{2,1,0:T(1,128)S(1)} all-gather(f32[1,1,128]{2,1,0:T(1,128)S(1)} %bitcast.102), channel_id=4, replica_groups=mesh['grp'=8,'vocab'=32] {'vocab'}, dimensions={0}, use_global_device_ids=true | all-gather | bytes 16896 | tf_op jit(solution)/shard_map/all_gather | solution.py:9
  345.3 27.2 %all-gather.7 = f32[32,1,128]{2,1,0:T(1,128)S(1)} all-gather(f32[1,1,128]{2,1,0:T(1,128)S(1)} %bitcast.101), channel_id=5, replica_groups=mesh['grp'=8,'vocab'=32] {'vocab'}, dimensions={0}, use_global_device_ids=true | all-gather | bytes 16896 | tf_op jit(solution)/shard_map/all_gather | solution.py:9
  372.5 2.7 while.21
  375.2 56.7 %psum.7 = f32[128]{0:T(128)S(1)} all-reduce(f32[128]{0:T(128)S(1)} %get-tuple-element.232), channel_id=1, replica_groups=mesh['grp'=8,'vocab'=32] {'vocab'}, use_global_device_ids=true, to_apply=%region_5.6 | all-reduce | flops 128 | bytes 1024 | tf_op jit(solution)/shard_map/psum | solution.py:111
  431.9 0.7 all_to_all.38
  432.6 54.2 %all-to-all-start.4 = ((f32[8,1,16]{2,1,0:T(1,128)}), f32[8,1,16]{2,1,0:T(1,128)S(1)}, u32[]{:S(2)}, u32[]{:S(2)}) async-start(f32[8,1,16]{2,1,0:T(1,128)} %bitcast.28), calls=%async_computation.5 | async-start | bytes 8192 | tf_op jit(solution)/shard_map/all_to_all | solution.py:113
  486.8 0.0 copy-done.2
  486.8 4.6 all-to-all-done.4
  491.4 0.5 broadcast.133
  491.9 0.7 reduce.7
  492.6 0.1 reshape.221
  492.7 1.0 scatter_custom_fusion.1
  493.7 0.2 select_reduce_fusion.2
  493.9 0.5 fusion.18
  (112 shorter events, 1.8 us)
Async XLA Ops:
  7.2 3.6 copy-start
  7.2 247.6 %reduce-scatter.2.cloned.1.call-start = ((), (), s32[]{:S(2)}) async-start(), calls=%async_computation.6 | async-start | bytes 9437184 | tf_op jit(solution)/shard_map/reduce_scatter | solution.py:98
  205.2 0.7 copy-start.1
  205.2 6.8 %copy-start.4 = (s32[1,8]{1,0:T(1,128)S(1)}, s32[1,8]{1,0:T(1,128)}, u32[]{:S(2)}) copy-start(s32[1,8]{1,0:T(1,128)} %param.11) | copy-start | bytes 100
  205.2 281.6 %copy-start.2 = (s32[128,1]{0,1:T(1,128)S(1)}, s32[128,1]{0,1:T(1,128)}, u32[]{:S(2)}) copy-start(s32[128,1]{0,1:T(1,128)} %param.8) | copy-start | bytes 1540
  207.8 8.8 %all-to-all-start = ((s32[8,1,16]{2,1,0:T(1,128)}), s32[8,1,16]{2,1,0:T(1,128)S(1)}, u32[]{:S(2)}, u32[]{:S(2)}) async-start(s32[8,1,16]{2,1,0:T(1,128)} %bitcast.7), calls=%async_computation | async-start | bytes 8192 | tf_op jit(solution)/shard_map/all_to_all | solution.py:95
  431.9 62.5 %copy-start.3 = (f32[128]{0:T(128)}, f32[128]{0:T(128)S(1)}, u32[]{:S(2)}) copy-start(f32[128]{0:T(128)S(1)} %compare_select_fusion.2) | copy-start | bytes 1540
  432.6 58.8 %all-to-all-start.4 = ((f32[8,1,16]{2,1,0:T(1,128)}), f32[8,1,16]{2,1,0:T(1,128)S(1)}, u32[]{:S(2)}, u32[]{:S(2)}) async-start(f32[8,1,16]{2,1,0:T(1,128)} %bitcast.28), calls=%async_computation.5 | async-start | bytes 8192 | tf_op jit(solution)/shard_map/all_to_all | solution.py:113
Sparse Core Ops, SparseCore 0:
  205.3 49.3 reduce-scatter.1
